TPU v7x, 512 devices: a whole 4x4x16 slice. The times are simulated.
512 devices in a mesh: view: 16 (over z_lo, y), tile: 32 (over x, z_hi, core).
Axes of the slice: x: 4, y: 4, z: 16 (z_hi: 4, z_lo: 4; z = z_hi * 4 + z_lo), core: 2. Of those that a mesh axis runs over, the one named last changes fastest.
Arguments:
- estimate: float32 [256, 256, 128], P('tile', 'view'), may hold values from 0.5 to 1.5
- images: float32 [16, 256, 256, 128], P('view', 'tile'), may hold values from 0.25 to 4
- taps_first: float32 [16, 5], P('view'), may hold values from 0.1 to 1
- taps_second: float32 [16, 7], P('view'), may hold values from 0.1 to 1
- taps_axial: float32 [16, 33], P('view'), may hold values from 0.02 to 0.2
Outputs:
- deconvolved: float32 [256, 256, 128], P('tile', 'view')
All inputs are finite; a program needn't handle non-finite values.
Results may differ from a plain program's by a relative error of at most 0.0001.
Values sent between devices are 32-bit elements; how exact they have to be, the bound alone decides.
No kernel may reach another device: no remote copies, remote signals or barrier semaphores. Data moves between devices by JAX's collectives and lax.ppermute only.
A program may use at most 64 MiB of HBM per device.

v0:
```python
import jax
import jax.numpy as jnp
from jax import lax
from jax.sharding import PartitionSpec as P

ITERS = 2


def extended(cells, sides, width):
    for axis, dim in sides:
        count = lax.axis_size(axis)
        ends = count - 1
        head = lax.slice_in_dim(cells, 0, width, axis=dim)
        tail = lax.slice_in_dim(cells, cells.shape[dim] - width, cells.shape[dim], axis=dim)
        cells = jnp.concatenate(
            [
                lax.ppermute(tail, axis, [(i, (i + 1) % count) for i in range(ends)]),
                cells,
                lax.ppermute(head, axis, [((i + 1) % count, i) for i in range(ends)]),
            ],
            axis=dim,
        )
    return cells


def toeplitz(taps, length, radius):
    index = jnp.arange(length, dtype=jnp.int32)
    offset = index[None, :] - index[:, None] + radius
    count = taps.shape[0]
    onehot = (offset[None, :, :] == jnp.arange(count, dtype=jnp.int32)[:, None, None]).astype(
        jnp.float32
    )
    return jnp.sum(onehot * taps[:, None, None], axis=0)


def along_axial(field, matrix):
    flat = field.reshape(-1, field.shape[2])
    out = jnp.dot(flat, matrix, precision=lax.Precision.HIGHEST, preferred_element_type=jnp.float32)
    return out.reshape(field.shape)


def along_second(field, taps, reverse):
    count = taps.shape[0]
    radius = (count - 1) // 2
    length = field.shape[1]
    padded = jnp.pad(field, ((0, 0), (radius, radius), (0, 0)))
    total = jnp.zeros(field.shape, jnp.float32)
    for tap in range(count):
        start = tap if reverse else 2 * radius - tap
        total = total + taps[tap] * padded[:, start : start + length, :]
    return total


def along_first(padded, taps, reverse):
    count = taps.shape[0]
    radius = (count - 1) // 2
    length = padded.shape[0] - 2 * radius
    total = jnp.zeros((length,) + padded.shape[1:], jnp.float32)
    for tap in range(count):
        start = tap if reverse else 2 * radius - tap
        total = total + taps[tap] * padded[start : start + length]
    return total


def spread(piece):
    return lax.all_gather(piece, "view", axis=1, tiled=True)


def local(estimate, images, taps_first, taps_second, taps_axial):
    first = taps_first[0]
    second = taps_second[0]
    axial = taps_axial[0]
    image = images[0]
    radius = (first.shape[0] - 1) // 2
    matrix = toeplitz(axial, estimate.shape[2], (axial.shape[0] - 1) // 2)
    views = lax.axis_size("view")
    width = estimate.shape[1]
    current = spread(estimate)
    for step in range(ITERS):
        inner = along_second(along_axial(current, matrix), second, False)
        blurred = along_first(extended(inner, (("tile", 0),), radius), first, False)
        ratio = image / blurred
        inner = along_second(along_axial(ratio, matrix.T), second, True)
        total = along_first(extended(inner, (("tile", 0),), radius), first, True)
        current = current * (lax.psum(total, "view") / views)
    own = lax.dynamic_slice_in_dim(current, lax.axis_index("view") * width, width, 1)
    return own


def solution(mesh):
    in_specs = (
        P("tile", "view", None),
        P("view", "tile", None, None),
        P("view", None),
        P("view", None),
        P("view", None),
    )
    out_specs = P("tile", "view", None)
    return jax.shard_map(local, mesh=mesh, in_specs=in_specs, out_specs=out_specs, check_vma=False)
```

profile of v0, /device:TPU:2, one launch (start us, length us, event | category | flops | bytes accessed | tf_op | source)
XLA Modules:
  0.0 563.0 jit_solution(5084498150551239331)
XLA Ops:
  7.3 1.5 fusion.79
  9.8 90.1 %all-gather.2.cloned.1.call-done = f32[8,256,128]{2,1,0:T(8,128)} async-done(((f32[8,16,128]{2,1,0:T(8,128)}), f32[8,256,128]{2,1,0:T(8,128)}) %all-gather.2.cloned.1.call-update) | async-done | bytes 1048592 | tf_op jit(solution)/shard_map/all_gather | solution.py:66
  99.9 2.3 convolution_bitcast_fusion
  102.5 5.0 multiply_add_fusion.3
  107.7 2.1 collective-permute-start
  109.7 2.4 collective-permute-start.1
  112.8 3.1 collective-permute-done
  115.9 10.1 %collective-permute-done.1 = f32[2,256,128]{2,1,0:T(8,128)S(1)} collective-permute-done((f32[2,256,128]{2,1,0:T(8,128)S(1)}, f32[2,256,128]{2,1,0:T(8,128)S(1)}, u32[]{:S(2)}, u32[]{:S(2)}) %collective-permute-start.1) | collective-permute-done | bytes 262176 | tf_op jit(solution)/shard_map/ppermute | solution.py:17
  126.0 4.4 fusion.54
  130.5 5.0 multiply_add_fusion.2
  135.6 1.9 collective-permute-start.2
  137.5 8.4 %collective-permute-start.3 = (f32[2,256,128]{2,1,0:T(8,128)S(1)}, f32[2,256,128]{2,1,0:T(8,128)S(1)}, u32[]{:S(2)}, u32[]{:S(2)}) collective-permute-start(f32[2,256,128]{2,1,0:T(8,128)S(1)} %get-tuple-element.10), channel_id=1, source_target_pairs={{1,0},{2,1},{3,2},{4,3},{5,4},{6,5},{7,6},{8,7},{9,8},{10,9},{11,1... | collective-permute-start | bytes 786440 | tf_op jit(solution)/shard_map/ppermute | solution.py:19
  146.0 4.2 collective-permute-done.2
  150.2 1.7 collective-permute-done.3
  151.9 4.5 fusion.20
  156.4 171.3 %all-reduce.7.cloned.1.call-done = f32[8,256,128]{2,1,0:T(8,128)} async-done(((f32[8,256,128]{2,1,0:T(8,128)}), f32[8,256,128]{2,1,0:T(8,128)}) %all-reduce.7.cloned.1.call-update) | async-done | bytes 1048592 | tf_op jit(solution)/shard_map/psum | solution.py:85
  327.8 1.3 multiply_multiply_fusion
  329.1 1.0 fusion.69
  330.1 5.0 multiply_add_fusion.1
  335.2 1.9 collective-permute-start.4
  337.1 2.4 collective-permute-start.5
  339.5 4.1 collective-permute-done.4
  343.6 9.3 %collective-permute-done.5 = f32[2,256,128]{2,1,0:T(8,128)S(1)} collective-permute-done((f32[2,256,128]{2,1,0:T(8,128)S(1)}, f32[2,256,128]{2,1,0:T(8,128)S(1)}, u32[]{:S(2)}, u32[]{:S(2)}) %collective-permute-start.5) | collective-permute-done | bytes 262176 | tf_op jit(solution)/shard_map/ppermute | solution.py:17
  352.9 4.4 fusion.56
  357.3 5.0 multiply_add_fusion
  362.4 1.9 collective-permute-start.6
  364.3 8.4 %collective-permute-start.7 = (f32[2,256,128]{2,1,0:T(8,128)S(1)}, f32[2,256,128]{2,1,0:T(8,128)S(1)}, u32[]{:S(2)}, u32[]{:S(2)}) collective-permute-start(f32[2,256,128]{2,1,0:T(8,128)S(1)} %get-tuple-element.6), channel_id=1, source_target_pairs={{1,0},{2,1},{3,2},{4,3},{5,4},{6,5},{7,6},{8,7},{9,8},{10,9},{11,1... | collective-permute-start | bytes 786440 | tf_op jit(solution)/shard_map/ppermute | solution.py:19
  372.8 3.8 collective-permute-done.6
  376.6 3.8 collective-permute-done.7
  380.4 4.5 fusion.3
  384.9 170.1 %all-reduce.9.cloned.1.call-done = f32[8,256,128]{2,1,0:T(8,128)} async-done(((f32[8,256,128]{2,1,0:T(8,128)}), f32[8,256,128]{2,1,0:T(8,128)}) %all-reduce.9.cloned.1.call-update) | async-done | bytes 1048592 | tf_op jit(solution)/shard_map/psum | solution.py:85
  555.0 1.5 dynamic-slice_multiply_fusion
  (20 shorter events, 2.9 us)
Async XLA Ops:
  6.5 93.4 %all-gather.2.cloned.1.call-start = ((), (), s32[]{:S(2)}) async-start(), calls=%async_computation | async-start | bytes 1114112 | tf_op jit(solution)/shard_map/all_gather | solution.py:66
  7.3 320.5 %all-reduce.7.cloned.1.call-start = ((), (), s32[]{:S(2)}) async-start(), calls=%async_computation.1 | async-start | bytes 2097152 | tf_op jit(solution)/shard_map/psum | solution.py:85
  107.6 4.5 copy-start.1
  107.6 18.4 %copy-start.2 = (f32[1,8,256,128]{3,2,1,0:T(8,128)S(1)}, f32[1,8,256,128]{3,2,1,0:T(8,128)}, u32[]{:S(2)}) copy-start(f32[1,8,256,128]{3,2,1,0:T(8,128)} %param.6) | copy-start | bytes 3145732
  107.7 8.3 %collective-permute-start = (f32[2,256,128]{2,1,0:T(8,128)S(1)}, f32[2,256,128]{2,1,0:T(8,128)S(1)}, u32[]{:S(2)}, u32[]{:S(2)}) collective-permute-start(f32[2,256,128]{2,1,0:T(8,128)S(1)} %get-tuple-element.11), channel_id=1, source_target_pairs={{1,0},{2,1},{3,2},{4,3},{5,4},{6,5},{7,6},{8,7},{9,8},{10,9},{11,1... | collective-permute-start | bytes 786440 | tf_op jit(solution)/shard_map/ppermute | solution.py:19
  109.7 16.3 %collective-permute-start.1 = (f32[2,256,128]{2,1,0:T(8,128)S(1)}, f32[2,256,128]{2,1,0:T(8,128)S(1)}, u32[]{:S(2)}, u32[]{:S(2)}) collective-permute-start(f32[2,256,128]{2,1,0:T(8,128)S(1)} %get-tuple-element.12), channel_id=1, source_target_pairs={{0,1},{1,2},{2,3},{3,4},{4,5},{5,6},{6,7},{7,8},{8,9},{9,10},{10,1... | collective-permute-start | bytes 786440 | tf_op jit(solution)/shard_map/ppermute | solution.py:17
  135.6 14.6 %collective-permute-start.2 = (f32[2,256,128]{2,1,0:T(8,128)S(1)}, f32[2,256,128]{2,1,0:T(8,128)S(1)}, u32[]{:S(2)}, u32[]{:S(2)}) collective-permute-start(f32[2,256,128]{2,1,0:T(8,128)S(1)} %get-tuple-element.9), channel_id=1, source_target_pairs={{0,1},{1,2},{2,3},{3,4},{4,5},{5,6},{6,7},{7,8},{8,9},{9,10},{10,1... | collective-permute-start | bytes 786440 | tf_op jit(solution)/shard_map/ppermute | solution.py:17
  137.5 14.4 %collective-permute-start.3 = (f32[2,256,128]{2,1,0:T(8,128)S(1)}, f32[2,256,128]{2,1,0:T(8,128)S(1)}, u32[]{:S(2)}, u32[]{:S(2)}) collective-permute-start(f32[2,256,128]{2,1,0:T(8,128)S(1)} %get-tuple-element.10), channel_id=1, source_target_pairs={{1,0},{2,1},{3,2},{4,3},{5,4},{6,5},{7,6},{8,7},{9,8},{10,9},{11,1... | collective-permute-start | bytes 786440 | tf_op jit(solution)/shard_map/ppermute | solution.py:19
  156.4 171.4 %copy-start = (f32[8,256,128]{2,1,0:T(8,128)S(1)}, f32[8,256,128]{2,1,0:T(8,128)}, u32[]{:S(2)}) copy-start(f32[8,256,128]{2,1,0:T(8,128)} %all-gather.2.cloned.1.call-done) | copy-start | bytes 3145732
  156.4 398.6 %all-reduce.9.cloned.1.call-start = ((), (), s32[]{:S(2)}) async-start(), calls=%async_computation.2 | async-start | bytes 2097152 | tf_op jit(solution)/shard_map/psum | solution.py:85
  335.2 8.4 %collective-permute-start.4 = (f32[2,256,128]{2,1,0:T(8,128)S(1)}, f32[2,256,128]{2,1,0:T(8,128)S(1)}, u32[]{:S(2)}, u32[]{:S(2)}) collective-permute-start(f32[2,256,128]{2,1,0:T(8,128)S(1)} %get-tuple-element.7), channel_id=1, source_target_pairs={{1,0},{2,1},{3,2},{4,3},{5,4},{6,5},{7,6},{8,7},{9,8},{10,9},{11,1... | collective-permute-start | bytes 786440 | tf_op jit(solution)/shard_map/ppermute | solution.py:19
  337.1 15.8 %collective-permute-start.5 = (f32[2,256,128]{2,1,0:T(8,128)S(1)}, f32[2,256,128]{2,1,0:T(8,128)S(1)}, u32[]{:S(2)}, u32[]{:S(2)}) collective-permute-start(f32[2,256,128]{2,1,0:T(8,128)S(1)} %get-tuple-element.8), channel_id=1, source_target_pairs={{0,1},{1,2},{2,3},{3,4},{4,5},{5,6},{6,7},{7,8},{8,9},{9,10},{10,1... | collective-permute-start | bytes 786440 | tf_op jit(solution)/shard_map/ppermute | solution.py:17
  362.4 14.2 %collective-permute-start.6 = (f32[2,256,128]{2,1,0:T(8,128)S(1)}, f32[2,256,128]{2,1,0:T(8,128)S(1)}, u32[]{:S(2)}, u32[]{:S(2)}) collective-permute-start(f32[2,256,128]{2,1,0:T(8,128)S(1)} %get-tuple-element.5), channel_id=1, source_target_pairs={{0,1},{1,2},{2,3},{3,4},{4,5},{5,6},{6,7},{7,8},{8,9},{9,10},{10,1... | collective-permute-start | bytes 786440 | tf_op jit(solution)/shard_map/ppermute | solution.py:17
  364.3 16.1 %collective-permute-start.7 = (f32[2,256,128]{2,1,0:T(8,128)S(1)}, f32[2,256,128]{2,1,0:T(8,128)S(1)}, u32[]{:S(2)}, u32[]{:S(2)}) collective-permute-start(f32[2,256,128]{2,1,0:T(8,128)S(1)} %get-tuple-element.6), channel_id=1, source_target_pairs={{1,0},{2,1},{3,2},{4,3},{5,4},{6,5},{7,6},{8,7},{9,8},{10,9},{11,1... | collective-permute-start | bytes 786440 | tf_op jit(solution)/shard_map/ppermute | solution.py:19
Sparse Core Ops, SparseCore 0:
  9.4 90.4 all-gather.1
  156.5 171.2 all-reduce.6
  385.0 169.9 all-reduce.8
where the time goes:
time: 564 us; the launch traced here: 563 us
  waiting for transfers between devices  472 us (84%)
  other arithmetic  32.9 us (6%)
  starting transfers between devices  29.6 us (5%)
  between operations  13.3 us (2%)
  matrix products  12.1 us (2%)
    psum x2, waiting for transfers between devices, local(): current = current * (lax.psum(total, 'view') / views)  341 us
    all_gather x1, waiting for transfers between devices, spread(): return lax.all_gather(piece, 'view', axis=1, tiled=True)  90.1 us
    ppermute x4, waiting for transfers between devices, extended(): lax.ppermute(tail, axis, [(i, (i + 1) % count) for i in range(ends)])  27.3 us
    ppermute x4, starting transfers between devices, extended(): lax.ppermute(head, axis, [((i + 1) % count, i) for i in range(ends)])  20.9 us
    add x4, other arithmetic, along_second(): total = total + taps[tap] * padded[:, start:start + length, :]  20.2 us
    ppermute x4, waiting for transfers between devices, extended(): lax.ppermute(head, axis, [((i + 1) % count, i) for i in range(ends)])  12.8 us
    dot_general x4, matrix products, along_axial(): jnp.dot(flat, matrix, precision=lax.Precision.HIGHEST, preferred_element_...  12.1 us
  transfers between devices with their start and end apart: 11, of which 11 were waited for; matrix products, arithmetic and copies ran while one was open for 1% of the time, Pallas kernels for 0%

commit v1 on v0

--- a/solution.py
+++ b/solution.py
@@ -63,7 +63,11 @@
 
 
 def spread(piece):
-    return lax.all_gather(piece, "view", axis=1, tiled=True)
+    order_leaves = lambda m: jnp.concatenate(
+        lax.all_to_all(jnp.stack([m for _ in range(lax.psum(1, "view"))], axis=0), "view", 0, 0),
+        axis=1,
+    )
+    return order_leaves(piece)
 
 
 def local(estimate, images, taps_first, taps_second, taps_axial):

time: 564 us -> 518 us (0.918)
  waiting for transfers between devices: 472 us -> 413 us
  starting transfers between devices: 29.6 us -> 42.9 us
    all_gather x1 -> x0, waiting for transfers between devices: 90.1 us -> none  [spread(): return lax.all_gather(piece, 'view', axis=1, tiled=True)]
    all_to_all x0 -> x1, waiting for transfers between devices: none -> 23.5 us  [spread(): lax.all_to_all(jnp.stack([m for _ in range(lax.psum(1, 'view'))], axis=0)...]
    psum x2, waiting for transfers between devices: 341 us -> 354 us  [local(): current = current * (lax.psum(total, 'view') / views)]
    all_to_all x0 -> x1, starting transfers between devices: none -> 8.77 us  [spread(): lax.all_to_all(jnp.stack([m for _ in range(lax.psum(1, 'view'))], axis=0)...]
  transfers between devices with their start and end apart: 11 -> 11, of which waited for: 11 -> 11; matrix products, arithmetic and copies ran while one was open for 1% -> 0% of each run, Pallas kernels for 0% -> 0%
where the time goes in v1:
time: 518 us; the launch traced here: 517 us
  waiting for transfers between devices  413 us (80%)
  starting transfers between devices  42.9 us (8%)
  other arithmetic  33 us (6%)
  between operations  13.6 us (3%)
  matrix products  10.9 us (2%)
    psum x2, waiting for transfers between devices, local(): current = current * (lax.psum(total, 'view') / views)  354 us
    ppermute x4, starting transfers between devices, extended(): lax.ppermute(head, axis, [((i + 1) % count, i) for i in range(ends)])  25.9 us
    ppermute x4, waiting for transfers between devices, extended(): lax.ppermute(tail, axis, [(i, (i + 1) % count) for i in range(ends)])  23.9 us
    all_to_all x1, waiting for transfers between devices, spread(): lax.all_to_all(jnp.stack([m for _ in range(lax.psum(1, 'view'))], axis=0)...  23.5 us
    add x4, other arithmetic, along_second(): total = total + taps[tap] * padded[:, start:start + length, :]  20.9 us
    ppermute x4, waiting for transfers between devices, extended(): lax.ppermute(head, axis, [((i + 1) % count, i) for i in range(ends)])  10.9 us
    dot_general x4, matrix products, along_axial(): jnp.dot(flat, matrix, precision=lax.Precision.HIGHEST, preferred_element_...  10.9 us
  transfers between devices with their start and end apart: 11, of which 11 were waited for; matrix products, arithmetic and copies ran while one was open for 0% of the time, Pallas kernels for 0%

profile of v1, /device:TPU:2, one launch (start us, length us, event | category | flops | bytes accessed | tf_op | source)
XLA Modules:
  0.0 517.0 jit_solution(2804108270566694373)
XLA Ops:
  6.5 1.9 stack.2
  8.5 8.8 %all-to-all-start = ((f32[16,8,16,128]{3,2,1,0:T(8,128)}), f32[16,8,16,128]{3,2,1,0:T(8,128)S(1)}, u32[]{:S(2)}, u32[]{:S(2)}) async-start(f32[16,8,16,128]{3,2,1,0:T(8,128)} %stack.2), calls=%async_computation | async-start | bytes 2097152 | tf_op jit(solution)/shard_map/all_to_all | solution.py:67
  18.3 23.5 %all-to-all-done = f32[16,8,16,128]{3,2,1,0:T(8,128)S(1)} async-done(((f32[16,8,16,128]{3,2,1,0:T(8,128)}), f32[16,8,16,128]{3,2,1,0:T(8,128)S(1)}, u32[]{:S(2)}, u32[]{:S(2)}) %all-to-all-start) | async-done | bytes 1048608 | tf_op jit(solution)/shard_map/all_to_all | solution.py:67
  41.9 1.1 convolution_bitcast_fusion
  43.3 5.2 %multiply_add_fusion.3 = f32[8,256,128]{2,1,0:T(8,128)S(1)} fusion(f32[8,256,128]{2,1,0:T(8,128)S(1)} %bitcast.38, f32[]{:T(128)} %bitcast.13, f32[]{:T(128)} %bitcast.12, f32[]{:T(128)} %bitcast.11, f32[]{:T(128)} %bitcast.10, f32[]{:T(128)} %bitcast.9, f32[]{:T(128)} %bitcast.8, f32[]{:T(128)} %bitcast.3), kind=kLoop, calls=%fused_computation.88 | loop fusion | flops 3407872 | bytes 2097180 | tf_op jit(solution)/shard_map/add | solution.py:50
  48.6 7.1 %collective-permute-start = (f32[2,256,128]{2,1,0:T(8,128)S(1)}, f32[2,256,128]{2,1,0:T(8,128)S(1)}, u32[]{:S(2)}, u32[]{:S(2)}) collective-permute-start(f32[2,256,128]{2,1,0:T(8,128)S(1)} %get-tuple-element.11), channel_id=1, source_target_pairs={{1,0},{2,1},{3,2},{4,3},{5,4},{6,5},{7,6},{8,7},{9,8},{10,9},{11,1... | collective-permute-start | bytes 786440 | tf_op jit(solution)/shard_map/ppermute | solution.py:19
  55.7 1.9 collective-permute-start.1
  58.3 1.3 collective-permute-done
  59.6 8.8 %collective-permute-done.1 = f32[2,256,128]{2,1,0:T(8,128)S(1)} collective-permute-done((f32[2,256,128]{2,1,0:T(8,128)S(1)}, f32[2,256,128]{2,1,0:T(8,128)S(1)}, u32[]{:S(2)}, u32[]{:S(2)}) %collective-permute-start.1) | collective-permute-done | bytes 262176 | tf_op jit(solution)/shard_map/ppermute | solution.py:17
  68.4 4.4 fusion.54
  72.8 5.2 %multiply_add_fusion.2 = f32[8,256,128]{2,1,0:T(8,128)S(1)} fusion(f32[8,256,128]{2,1,0:T(8,128)S(1)} %fusion.54, f32[]{:T(128)} %bitcast.13, f32[]{:T(128)} %bitcast.12, f32[]{:T(128)} %bitcast.11, f32[]{:T(128)} %bitcast.10, f32[]{:T(128)} %bitcast.9, f32[]{:T(128)} %bitcast.8, f32[]{:T(128)} %bitcast.3), kind=kLoop, calls=%fused_computation.82 | loop fusion | flops 3407872 | bytes 2097180 | tf_op jit(solution)/shard_map/add | solution.py:50
  78.1 1.9 collective-permute-start.2
  80.0 8.4 %collective-permute-start.3 = (f32[2,256,128]{2,1,0:T(8,128)S(1)}, f32[2,256,128]{2,1,0:T(8,128)S(1)}, u32[]{:S(2)}, u32[]{:S(2)}) collective-permute-start(f32[2,256,128]{2,1,0:T(8,128)S(1)} %get-tuple-element.10), channel_id=1, source_target_pairs={{1,0},{2,1},{3,2},{4,3},{5,4},{6,5},{7,6},{8,7},{9,8},{10,9},{11,1... | collective-permute-start | bytes 786440 | tf_op jit(solution)/shard_map/ppermute | solution.py:19
  88.5 2.1 collective-permute-done.2
  90.6 1.8 collective-permute-done.3
  92.3 4.5 fusion.20
  96.9 184.2 %all-reduce.7.cloned.1.call-done = f32[8,256,128]{2,1,0:T(8,128)} async-done(((f32[8,256,128]{2,1,0:T(8,128)}), f32[8,256,128]{2,1,0:T(8,128)}) %all-reduce.7.cloned.1.call-update) | async-done | bytes 1048592 | tf_op jit(solution)/shard_map/psum | solution.py:89
  281.1 1.4 bitcast_multiply_fusion
  283.5 5.2 %multiply_add_fusion.1 = f32[8,256,128]{2,1,0:T(8,128)S(1)} fusion(f32[8,256,128]{2,1,0:T(8,128)S(1)} %fusion.69, f32[]{:T(128)} %bitcast.13, f32[]{:T(128)} %bitcast.12, f32[]{:T(128)} %bitcast.11, f32[]{:T(128)} %bitcast.10, f32[]{:T(128)} %bitcast.9, f32[]{:T(128)} %bitcast.8, f32[]{:T(128)} %bitcast.3), kind=kLoop, calls=%fused_computation.76 | loop fusion | flops 3407872 | bytes 2097180 | tf_op jit(solution)/shard_map/add | solution.py:50
  288.7 1.9 collective-permute-start.4
  290.7 2.4 collective-permute-start.5
  293.1 4.1 collective-permute-done.4
  297.2 9.3 %collective-permute-done.5 = f32[2,256,128]{2,1,0:T(8,128)S(1)} collective-permute-done((f32[2,256,128]{2,1,0:T(8,128)S(1)}, f32[2,256,128]{2,1,0:T(8,128)S(1)}, u32[]{:S(2)}, u32[]{:S(2)}) %collective-permute-start.5) | collective-permute-done | bytes 262176 | tf_op jit(solution)/shard_map/ppermute | solution.py:17
  306.4 4.4 fusion.56
  310.9 5.2 %multiply_add_fusion = f32[8,256,128]{2,1,0:T(8,128)S(1)} fusion(f32[8,256,128]{2,1,0:T(8,128)S(1)} %fusion.56, f32[]{:T(128)} %bitcast.13, f32[]{:T(128)} %bitcast.12, f32[]{:T(128)} %bitcast.11, f32[]{:T(128)} %bitcast.10, f32[]{:T(128)} %bitcast.9, f32[]{:T(128)} %bitcast.8, f32[]{:T(128)} %bitcast.3), kind=kLoop, calls=%fused_computation.70 | loop fusion | flops 3407872 | bytes 2097180 | tf_op jit(solution)/shard_map/add | solution.py:50
  316.1 1.9 collective-permute-start.6
  318.1 8.4 %collective-permute-start.7 = (f32[2,256,128]{2,1,0:T(8,128)S(1)}, f32[2,256,128]{2,1,0:T(8,128)S(1)}, u32[]{:S(2)}, u32[]{:S(2)}) collective-permute-start(f32[2,256,128]{2,1,0:T(8,128)S(1)} %get-tuple-element.6), channel_id=1, source_target_pairs={{1,0},{2,1},{3,2},{4,3},{5,4},{6,5},{7,6},{8,7},{9,8},{10,9},{11,1... | collective-permute-start | bytes 786440 | tf_op jit(solution)/shard_map/ppermute | solution.py:19
  326.5 3.8 collective-permute-done.6
  330.3 3.9 collective-permute-done.7
  334.1 4.5 fusion.3
  338.7 170.0 %all-reduce.9.cloned.1.call-done = f32[8,256,128]{2,1,0:T(8,128)} async-done(((f32[8,256,128]{2,1,0:T(8,128)}), f32[8,256,128]{2,1,0:T(8,128)}) %all-reduce.9.cloned.1.call-update) | async-done | bytes 1048592 | tf_op jit(solution)/shard_map/psum | solution.py:89
  508.7 1.5 dynamic-slice_multiply_fusion
  (23 shorter events, 3.3 us)
Async XLA Ops:
  8.5 8.8 %copy-start = (f32[1,7]{1,0:T(1,128)S(1)}, f32[1,7]{1,0:T(1,128)}, u32[]{:S(2)}) copy-start(f32[1,7]{1,0:T(1,128)} %param.8) | copy-start | bytes 88
  8.5 9.5 %copy-start.2 = (f32[1,33]{1,0:T(1,128)S(1)}, f32[1,33]{1,0:T(1,128)}, u32[]{:S(2)}) copy-start(f32[1,33]{1,0:T(1,128)} %param.9) | copy-start | bytes 400
  8.5 33.3 %all-to-all-start = ((f32[16,8,16,128]{3,2,1,0:T(8,128)}), f32[16,8,16,128]{3,2,1,0:T(8,128)S(1)}, u32[]{:S(2)}, u32[]{:S(2)}) async-start(f32[16,8,16,128]{3,2,1,0:T(8,128)} %stack.2), calls=%async_computation | async-start | bytes 2097152 | tf_op jit(solution)/shard_map/all_to_all | solution.py:67
  17.2 263.9 %all-reduce.7.cloned.1.call-start = ((), (), s32[]{:S(2)}) async-start(), calls=%async_computation.1 | async-start | bytes 2097152 | tf_op jit(solution)/shard_map/psum | solution.py:89
  48.6 9.1 %copy-start.1 = (f32[1,5]{1,0:T(1,128)S(1)}, f32[1,5]{1,0:T(1,128)}, u32[]{:S(2)}) copy-start(f32[1,5]{1,0:T(1,128)} %param.7) | copy-start | bytes 64
  48.6 19.8 %copy-start.3 = (f32[1,8,256,128]{3,2,1,0:T(8,128)S(1)}, f32[1,8,256,128]{3,2,1,0:T(8,128)}, u32[]{:S(2)}) copy-start(f32[1,8,256,128]{3,2,1,0:T(8,128)} %param.6) | copy-start | bytes 3145732
  48.6 11.0 %collective-permute-start = (f32[2,256,128]{2,1,0:T(8,128)S(1)}, f32[2,256,128]{2,1,0:T(8,128)S(1)}, u32[]{:S(2)}, u32[]{:S(2)}) collective-permute-start(f32[2,256,128]{2,1,0:T(8,128)S(1)} %get-tuple-element.11), channel_id=1, source_target_pairs={{1,0},{2,1},{3,2},{4,3},{5,4},{6,5},{7,6},{8,7},{9,8},{10,9},{11,1... | collective-permute-start | bytes 786440 | tf_op jit(solution)/shard_map/ppermute | solution.py:19
  55.7 12.6 %collective-permute-start.1 = (f32[2,256,128]{2,1,0:T(8,128)S(1)}, f32[2,256,128]{2,1,0:T(8,128)S(1)}, u32[]{:S(2)}, u32[]{:S(2)}) collective-permute-start(f32[2,256,128]{2,1,0:T(8,128)S(1)} %get-tuple-element.12), channel_id=1, source_target_pairs={{0,1},{1,2},{2,3},{3,4},{4,5},{5,6},{6,7},{7,8},{8,9},{9,10},{10,1... | collective-permute-start | bytes 786440 | tf_op jit(solution)/shard_map/ppermute | solution.py:17
  78.1 12.5 %collective-permute-start.2 = (f32[2,256,128]{2,1,0:T(8,128)S(1)}, f32[2,256,128]{2,1,0:T(8,128)S(1)}, u32[]{:S(2)}, u32[]{:S(2)}) collective-permute-start(f32[2,256,128]{2,1,0:T(8,128)S(1)} %get-tuple-element.9), channel_id=1, source_target_pairs={{0,1},{1,2},{2,3},{3,4},{4,5},{5,6},{6,7},{7,8},{8,9},{9,10},{10,1... | collective-permute-start | bytes 786440 | tf_op jit(solution)/shard_map/ppermute | solution.py:17
  80.0 12.3 %collective-permute-start.3 = (f32[2,256,128]{2,1,0:T(8,128)S(1)}, f32[2,256,128]{2,1,0:T(8,128)S(1)}, u32[]{:S(2)}, u32[]{:S(2)}) collective-permute-start(f32[2,256,128]{2,1,0:T(8,128)S(1)} %get-tuple-element.10), channel_id=1, source_target_pairs={{1,0},{2,1},{3,2},{4,3},{5,4},{6,5},{7,6},{8,7},{9,8},{10,9},{11,1... | collective-permute-start | bytes 786440 | tf_op jit(solution)/shard_map/ppermute | solution.py:19
  96.8 411.8 %all-reduce.9.cloned.1.call-start = ((), (), s32[]{:S(2)}) async-start(), calls=%async_computation.2 | async-start | bytes 2097152 | tf_op jit(solution)/shard_map/psum | solution.py:89
  288.7 8.4 %collective-permute-start.4 = (f32[2,256,128]{2,1,0:T(8,128)S(1)}, f32[2,256,128]{2,1,0:T(8,128)S(1)}, u32[]{:S(2)}, u32[]{:S(2)}) collective-permute-start(f32[2,256,128]{2,1,0:T(8,128)S(1)} %get-tuple-element.7), channel_id=1, source_target_pairs={{1,0},{2,1},{3,2},{4,3},{5,4},{6,5},{7,6},{8,7},{9,8},{10,9},{11,1... | collective-permute-start | bytes 786440 | tf_op jit(solution)/shard_map/ppermute | solution.py:19
  290.7 15.8 %collective-permute-start.5 = (f32[2,256,128]{2,1,0:T(8,128)S(1)}, f32[2,256,128]{2,1,0:T(8,128)S(1)}, u32[]{:S(2)}, u32[]{:S(2)}) collective-permute-start(f32[2,256,128]{2,1,0:T(8,128)S(1)} %get-tuple-element.8), channel_id=1, source_target_pairs={{0,1},{1,2},{2,3},{3,4},{4,5},{5,6},{6,7},{7,8},{8,9},{9,10},{10,1... | collective-permute-start | bytes 786440 | tf_op jit(solution)/shard_map/ppermute | solution.py:17
  316.1 14.1 %collective-permute-start.6 = (f32[2,256,128]{2,1,0:T(8,128)S(1)}, f32[2,256,128]{2,1,0:T(8,128)S(1)}, u32[]{:S(2)}, u32[]{:S(2)}) collective-permute-start(f32[2,256,128]{2,1,0:T(8,128)S(1)} %get-tuple-element.5), channel_id=1, source_target_pairs={{0,1},{1,2},{2,3},{3,4},{4,5},{5,6},{6,7},{7,8},{8,9},{9,10},{10,1... | collective-permute-start | bytes 786440 | tf_op jit(solution)/shard_map/ppermute | solution.py:17
  318.1 16.1 %collective-permute-start.7 = (f32[2,256,128]{2,1,0:T(8,128)S(1)}, f32[2,256,128]{2,1,0:T(8,128)S(1)}, u32[]{:S(2)}, u32[]{:S(2)}) collective-permute-start(f32[2,256,128]{2,1,0:T(8,128)S(1)} %get-tuple-element.6), channel_id=1, source_target_pairs={{1,0},{2,1},{3,2},{4,3},{5,4},{6,5},{7,6},{8,7},{9,8},{10,9},{11,1... | collective-permute-start | bytes 786440 | tf_op jit(solution)/shard_map/ppermute | solution.py:19
Sparse Core Ops, SparseCore 0:
  97.0 184.1 all-reduce.6
  338.8 169.8 all-reduce.8
